TPU v7x, 32 devices: a whole 2x2x4 slice. The times are simulated.
32 devices in a mesh: rows: 8 (over z, y), rhs: 4 (over x, core).
Axes of the slice: x: 2, y: 2, z: 4, core: 2. Of those that a mesh axis runs over, the one named last changes fastest.
Arguments:
- right_sides: bfloat16 [65536, 1024], P(None, ('rows', 'rhs')), may hold values from -6 to 6
- col_panels: bfloat16 [2, 65536, 1024], P(None, ('rows', 'rhs')), may hold values from -0.1875 to 0.1875
- diag_inverses: bfloat16 [2, 1024, 1024], replicated, may hold values from -0.1875 to 0.1875
Outputs:
- current: float32 [65536, 1024], P(('rows', 'rhs'))
All inputs are finite; a program needn't handle non-finite values.
Results may differ from a plain program's by a relative error of at most 0.003.
Values may be sent and summed in bfloat16 or wider, within the bound.
No kernel may reach another device: no remote copies, remote signals or barrier semaphores. Data moves between devices by JAX's collectives and lax.ppermute only.
A program may use at most 128 MiB of HBM per device.

v0:
```python
import jax
import jax.numpy as jnp
from jax import lax
from jax.sharding import PartitionSpec as P


def spread(shard, axis, root):
    mine = lax.axis_index(axis) == root
    return lax.psum(jnp.where(mine, shard, jnp.zeros_like(shard)), axis)


def local(right_sides, col_panels, diag_inverses):
    panel_size = diag_inverses.shape[1]
    early_solved = None
    gathered = lax.all_to_all(right_sides, ("rows", "rhs"), split_axis=0, concat_axis=1, tiled=True)
    current = gathered.astype(jnp.float32)
    rows_dev = current.shape[0]
    panel_count = diag_inverses.shape[0]
    devices_all = lax.axis_size("rows") * lax.axis_size("rhs")
    position = lax.axis_index(("rows", "rhs"))
    global_rows = position * rows_dev + jnp.arange(rows_dev, dtype=jnp.int32)
    for panel_id in range(panel_count):
        owner_dev = panel_id * devices_all // panel_count
        first_row = owner_dev * rows_dev
        is_owner = position == owner_dev
        local_panel = current[:panel_size].astype(jnp.bfloat16)
        inverse_now = diag_inverses[panel_id]
        solved_here = lax.cond(
            is_owner,
            lambda: jnp.dot(inverse_now, local_panel, preferred_element_type=jnp.float32).astype(
                jnp.bfloat16
            ),
            lambda: jnp.zeros(local_panel.shape, jnp.bfloat16),
        )
        solved = spread(solved_here, ("rows", "rhs"), owner_dev)
        update_term = jnp.dot(col_panels[panel_id], solved, preferred_element_type=jnp.float32)
        trailing = (global_rows >= first_row + panel_size)[:, None]
        current = jnp.where(trailing, current - update_term, current)
        top_rows = jnp.where(is_owner, solved.astype(jnp.float32), current[:panel_size])
        current = jnp.concatenate([top_rows, current[panel_size:]], axis=0)
    return current


def solution(mesh):
    return jax.shard_map(
        local,
        mesh=mesh,
        in_specs=(P(None, ("rows", "rhs")), P(None, ("rows", "rhs"), None), P()),
        out_specs=P(("rows", "rhs"), None),
        check_vma=False,
    )
```

profile of v0, /device:TPU:0, one launch (start us, length us, event | category | flops | bytes accessed | tf_op | source)
XLA Modules:
  0.0 446.5 jit_solution(2553022597957633385)
XLA Ops:
  6.5 4.8 %copy.27 = bf16[4,32,8,2048]{3,2,0,1:T(8,128)(2,1)} copy(bf16[4,32,8,2048]{3,2,1,0:T(8,128)(2,1)} %bitcast.34) | data formatting | bytes 8388608 | tf_op jit(solution)/shard_map/all_to_all | solution.py:15
  11.3 7.4 %all-to-all-start = ((bf16[32,2048,32]{1,2,0:T(8,128)(2,1)}), bf16[32,2048,32]{1,2,0:T(8,128)(2,1)}, u32[]{:S(2)}, u32[]{:S(2)}) async-start(bf16[32,2048,32]{1,2,0:T(8,128)(2,1)} %bitcast.33), calls=%async_computation | async-start | bytes 8388608 | tf_op jit(solution)/shard_map/all_to_all | solution.py:15
  18.8 0.0 all-reduce.3.cloned.1.call-start
  18.8 93.8 %all-to-all-done = bf16[32,2048,32]{1,2,0:T(8,128)(2,1)} async-done(((bf16[32,2048,32]{1,2,0:T(8,128)(2,1)}), bf16[32,2048,32]{1,2,0:T(8,128)(2,1)}, u32[]{:S(2)}, u32[]{:S(2)}) %all-to-all-start) | async-done | bytes 4194336 | tf_op jit(solution)/shard_map/all_to_all | solution.py:15
  112.6 9.4 %conditional.2 = (bf16[1024,1024]{0,1:T(8,128)(2,1)S(1)}) conditional(s32[]{:T(128)} %convert_element_type.35, () %tuple.18, (bf16[2,1024,1024]{2,1,0:T(8,128)(2,1)}, bf16[2048,32,32]{0,2,1:T(8,128)(2,1)}) %tuple.19), branch_computations={%region_0.0_spmd, %region_1.0_spmd} | conditional | flops 2148532224 | bytes 31457316 | solution.py:28
  112.6 2.0 slice.38
  114.6 0.9 copy-done.2
  115.4 3.7 fusion.3
  119.1 2.9 copy.22
  122.0 1.5 broadcast_select_fusion
  123.5 0.0 all-reduce.3.cloned.1.call-update
  123.5 0.0 all-reduce.5.cloned.1.call-start
  123.6 129.8 %all-reduce.3.cloned.1.call-done = bf16[1024,1024]{0,1:T(8,128)(2,1)} async-done(((bf16[1024,1024]{0,1:T(8,128)(2,1)}), bf16[1024,1024]{0,1:T(8,128)(2,1)}) %all-reduce.3.cloned.1.call-update) | async-done | bytes 2097168 | tf_op jit(solution)/shard_map/psum | solution.py:9
  253.3 8.7 %subtract_select_fusion.1 = f32[2048,1024]{0,1:T(8,128)S(1)} fusion(bf16[2048,1024]{0,1:T(8,128)(2,1)} %bitcast.9, bf16[1024,1024]{0,1:T(8,128)(2,1)} %all-reduce.3.cloned.1.call-done, bf16[2,2048,1024]{2,1,0:T(8,128)(2,1)} %param.8, pred[2048]{0:T(1024)(128)(4,1)S(1)} %fusion.17), kind=kOutput, calls=%fused_computation.9 | convolution fusion | flops 4301258752 | bytes 18876416 | tf_op jit(solution)/shard_map/dot_general | solution.py:36
  262.1 4.9 %fusion.18 = (bf16[1024,1024]{0,1:T(8,128)(2,1)}, f32[1024,1024]{0,1:T(8,128)}, f32[1024,1024]{0,1:T(8,128)}) fusion(f32[2048,1024]{0,1:T(8,128)S(1)} %subtract_select_fusion.1, bf16[1024,1024]{0,1:T(8,128)(2,1)S(1)} %copy-done, pred[]{:T(512)S(6)} %eq.9), kind=kLoop, calls=%fused_computation.23 | loop fusion | flops 3145728 | bytes 20971520 | tf_op jit(solution)/shard_map/convert_element_type | solution.py:26
  266.9 0.4 conditional.3
  266.9 0.3 broadcast.22.clone
  267.4 1.5 broadcast_select_fusion.1
  268.9 0.0 all-reduce.5.cloned.1.call-update
  268.9 139.6 %all-reduce.5.cloned.1.call-done = bf16[1024,1024]{0,1:T(8,128)(2,1)} async-done(((bf16[1024,1024]{0,1:T(8,128)(2,1)}), bf16[1024,1024]{0,1:T(8,128)(2,1)}) %all-reduce.5.cloned.1.call-update) | async-done | bytes 2097168 | tf_op jit(solution)/shard_map/psum | solution.py:9
  408.5 13.3 %subtract_select_fusion = f32[2048,1024]{0,1:T(8,128)} fusion(f32[1024,1024]{0,1:T(8,128)} %get-tuple-element.43, f32[1024,1024]{0,1:T(8,128)} %get-tuple-element.40, bf16[1024,1024]{0,1:T(8,128)(2,1)} %all-reduce.5.cloned.1.call-done, bf16[2,2048,1024]{2,1,0:T(8,128)(2,1)} %param.8, pred[2048]{0:T(1024)(128)(4,1)S(1)} %fusion.16), kind=kOutput, calls=%fused_computation.8 | convolution fusion | flops 4301258752 | bytes 23070720 | tf_op jit(solution)/shard_map/dot_general | solution.py:36
  421.9 4.7 %slice_select_fusion = (f32[1024,1024]{0,1:T(8,128)S(1)}, f32[1024,1024]{0,1:T(8,128)S(1)}) fusion(f32[2048,1024]{0,1:T(8,128)} %subtract_select_fusion, bf16[1024,1024]{0,1:T(8,128)(2,1)S(1)} %copy-done.1, pred[]{:T(512)S(6)} %eq.8), kind=kLoop, calls=%fused_computation.12 | loop fusion | flops 2097152 | bytes 18874368 | tf_op jit(solution)/shard_map/jit(_where)/select_n | solution.py:39
  426.6 3.8 pad_maximum_fusion
  430.4 9.2 %copy.19 = f32[2048,1024]{1,0:T(8,128)} copy(f32[2048,1024]{0,1:T(8,128)} %pad_maximum_fusion) | data formatting | bytes 16777216 | tf_op jit(solution)/shard_map/concatenate | solution.py:40
  (7 shorter events, 0.0 us)
Async XLA Ops:
  11.3 101.3 %all-to-all-start = ((bf16[32,2048,32]{1,2,0:T(8,128)(2,1)}), bf16[32,2048,32]{1,2,0:T(8,128)(2,1)}, u32[]{:S(2)}, u32[]{:S(2)}) async-start(bf16[32,2048,32]{1,2,0:T(8,128)(2,1)} %bitcast.33), calls=%async_computation | async-start | bytes 8388608 | tf_op jit(solution)/shard_map/all_to_all | solution.py:15
  18.8 234.6 %all-reduce.3.cloned.1.call-start = ((), (), s32[]{:S(2)}) async-start(), calls=%async_computation.1 | async-start | bytes 4194304 | tf_op jit(solution)/shard_map/psum | solution.py:9
  112.6 2.8 copy-start.2
  123.5 285.1 %all-reduce.5.cloned.1.call-start = ((), (), s32[]{:S(2)}) async-start(), calls=%async_computation.2 | async-start | bytes 4194304 | tf_op jit(solution)/shard_map/psum | solution.py:9
  253.3 8.8 %copy-start = (bf16[1024,1024]{0,1:T(8,128)(2,1)S(1)}, bf16[1024,1024]{0,1:T(8,128)(2,1)}, u32[]{:S(2)}) copy-start(bf16[1024,1024]{0,1:T(8,128)(2,1)} %all-reduce.3.cloned.1.call-done) | copy-start | bytes 6291460
  408.5 13.3 %copy-start.1 = (bf16[1024,1024]{0,1:T(8,128)(2,1)S(1)}, bf16[1024,1024]{0,1:T(8,128)(2,1)}, u32[]{:S(2)}) copy-start(bf16[1024,1024]{0,1:T(8,128)(2,1)} %all-reduce.5.cloned.1.call-done) | copy-start | bytes 6291460
Sparse Core Ops, SparseCore 0:
  123.6 129.6 all-reduce.2
  269.0 139.4 all-reduce.4
where the time goes:
time: 447 us; the launch traced here: 446 us
  waiting for transfers between devices  363 us (81%)
  matrix products  25.7 us (6%)
  local copies, waits for them, and re-layouts  19.9 us (4%)
  other arithmetic  16.4 us (4%)
  between operations  13.5 us (3%)
  starting transfers between devices  7.51 us (2%)
    psum x2, waiting for transfers between devices, spread(): return lax.psum(jnp.where(mine, shard, jnp.zeros_like(shard)), axis)  269 us
    all_to_all x1, waiting for transfers between devices, local(): lax.all_to_all(right_sides, ('rows', 'rhs'), split_axis=0, concat_axis=1,...  93.8 us
    dot_general x2, matrix products, local(): jnp.dot(col_panels[panel_id], solved, preferred_element_type=jnp.float32)  22 us
    concatenate x1, local copies, waits for them, and re-layouts, local(): current = jnp.concatenate([top_rows, current[panel_size:]], axis=0)  9.24 us
  transfers between devices with their start and end apart: 3, of which 3 were waited for; matrix products, arithmetic and copies ran while one was open for 0% of the time, Pallas kernels for 0%

commit v1 on v0

--- a/solution.py
+++ b/solution.py
@@ -12,7 +12,15 @@
 def local(right_sides, col_panels, diag_inverses):
     panel_size = diag_inverses.shape[1]
     early_solved = None
-    gathered = lax.all_to_all(right_sides, ("rows", "rhs"), split_axis=0, concat_axis=1, tiled=True)
+    gathered = jnp.concatenate(
+        lax.all_to_all(
+            jnp.stack(jnp.split(right_sides, lax.axis_size(("rows", "rhs")), axis=0)),
+            ("rows", "rhs"),
+            0,
+            0,
+        ),
+        axis=1,
+    )
     current = gathered.astype(jnp.float32)
     rows_dev = current.shape[0]
     panel_count = diag_inverses.shape[0]

time: 447 us -> 493 us (1.10)
  local copies, waits for them, and re-layouts: 19.9 us -> 65.3 us
    unnamed x4 -> x35, local copies, waits for them, and re-layouts: 0.01 us -> 48.6 us
where the time goes in v1:
time: 493 us; the launch traced here: 492 us
  waiting for transfers between devices  363 us (74%)
  local copies, waits for them, and re-layouts  65.3 us (13%)
  matrix products  25.7 us (5%)
  other arithmetic  16.4 us (3%)
  between operations  13.5 us (3%)
  starting transfers between devices  7.51 us (2%)
    psum x2, waiting for transfers between devices, spread(): return lax.psum(jnp.where(mine, shard, jnp.zeros_like(shard)), axis)  269 us
    all_to_all x1, waiting for transfers between devices, local(): lax.all_to_all(jnp.stack(jnp.split(right_sides, lax.axis_size(('rows', 'r...  93.8 us
    unnamed x35, local copies, waits for them, and re-layouts  48.6 us
    dot_general x2, matrix products, local(): jnp.dot(col_panels[panel_id], solved, preferred_element_type=jnp.float32)  22 us
  transfers between devices with their start and end apart: 3, of which 3 were waited for; matrix products, arithmetic and copies ran while one was open for 0% of the time, Pallas kernels for 0%

profile of v1, /device:TPU:0, one launch (start us, length us, event | category | flops | bytes accessed | tf_op | source)
XLA Modules:
  0.0 491.8 jit_solution(14525344205852373317)
XLA Ops:
  6.5 1.6 bitcast_dynamic-update-slice_fusion.31
  8.1 1.6 bitcast_dynamic-update-slice_fusion.30
  9.7 1.6 bitcast_dynamic-update-slice_fusion.29
  11.2 1.6 bitcast_dynamic-update-slice_fusion.28
  12.8 1.6 bitcast_dynamic-update-slice_fusion.27
  14.4 1.6 bitcast_dynamic-update-slice_fusion.26
  15.9 1.6 bitcast_dynamic-update-slice_fusion.25
  23.8 1.6 bitcast_dynamic-update-slice_fusion.20
  34.7 1.6 bitcast_dynamic-update-slice_fusion.13
  53.6 1.6 bitcast_dynamic-update-slice_fusion.1
  56.7 7.4 %all-to-all-start = ((bf16[32,2048,32]{1,2,0:T(8,128)(2,1)}), bf16[32,2048,32]{1,2,0:T(8,128)(2,1)}, u32[]{:S(2)}, u32[]{:S(2)}) async-start(bf16[32,2048,32]{1,2,0:T(8,128)(2,1)} %bitcast_dynamic-update-slice_fusion), calls=%async_computation | async-start | bytes 8388608 | tf_op jit(solution)/shard_map/all_to_all | solution.py:16
  64.2 93.8 %all-to-all-done = bf16[32,2048,32]{1,2,0:T(8,128)(2,1)} async-done(((bf16[32,2048,32]{1,2,0:T(8,128)(2,1)}), bf16[32,2048,32]{1,2,0:T(8,128)(2,1)}, u32[]{:S(2)}, u32[]{:S(2)}) %all-to-all-start) | async-done | bytes 4194336 | tf_op jit(solution)/shard_map/all_to_all | solution.py:16
  158.0 9.4 %conditional.2 = (bf16[1024,1024]{0,1:T(8,128)(2,1)S(1)}) conditional(s32[]{:T(128)} %convert_element_type.35, () %tuple.18, (bf16[2,1024,1024]{2,1,0:T(8,128)(2,1)}, bf16[2048,32,32]{0,2,1:T(8,128)(2,1)}) %tuple.19), branch_computations={%region_0.0_spmd, %region_1.0_spmd} | conditional | flops 2148532224 | bytes 31457316 | solution.py:36
  158.0 2.0 slice.38
  160.8 3.7 fusion.3
  164.5 2.9 copy.47
  168.9 129.8 %all-reduce.3.cloned.1.call-done = bf16[1024,1024]{0,1:T(8,128)(2,1)} async-done(((bf16[1024,1024]{0,1:T(8,128)(2,1)}), bf16[1024,1024]{0,1:T(8,128)(2,1)}) %all-reduce.3.cloned.1.call-update) | async-done | bytes 2097168 | tf_op jit(solution)/shard_map/psum | solution.py:9
  298.7 8.7 %subtract_select_fusion.1 = f32[2048,1024]{0,1:T(8,128)S(1)} fusion(bf16[2048,1024]{0,1:T(8,128)(2,1)} %bitcast.41, bf16[1024,1024]{0,1:T(8,128)(2,1)} %all-reduce.3.cloned.1.call-done, bf16[2,2048,1024]{2,1,0:T(8,128)(2,1)} %param.8, pred[2048]{0:T(1024)(128)(4,1)S(1)} %fusion.17), kind=kOutput, calls=%fused_computation.9 | convolution fusion | flops 4301258752 | bytes 18876416 | tf_op jit(solution)/shard_map/dot_general | solution.py:44
  307.4 4.9 fusion.18
  314.3 139.6 %all-reduce.5.cloned.1.call-done = bf16[1024,1024]{0,1:T(8,128)(2,1)} async-done(((bf16[1024,1024]{0,1:T(8,128)(2,1)}), bf16[1024,1024]{0,1:T(8,128)(2,1)}) %all-reduce.5.cloned.1.call-update) | async-done | bytes 2097168 | tf_op jit(solution)/shard_map/psum | solution.py:9
  453.9 13.3 %subtract_select_fusion = f32[2048,1024]{0,1:T(8,128)} fusion(f32[1024,1024]{0,1:T(8,128)} %get-tuple-element.39, f32[1024,1024]{0,1:T(8,128)} %get-tuple-element.36, bf16[1024,1024]{0,1:T(8,128)(2,1)} %all-reduce.5.cloned.1.call-done, bf16[2,2048,1024]{2,1,0:T(8,128)(2,1)} %param.8, pred[2048]{0:T(1024)(128)(4,1)S(1)} %fusion.16), kind=kOutput, calls=%fused_computation.8 | convolution fusion | flops 4301258752 | bytes 23070720 | tf_op jit(solution)/shard_map/dot_general | solution.py:44
  467.2 4.7 slice_select_fusion
  471.9 3.8 pad_maximum_fusion
  475.7 9.2 %copy.44 = f32[2048,1024]{1,0:T(8,128)} copy(f32[2048,1024]{0,1:T(8,128)} %pad_maximum_fusion) | data formatting | bytes 16777216 | tf_op jit(solution)/shard_map/concatenate | solution.py:48
  (38 shorter events, 39.1 us)
Async XLA Ops:
  56.7 101.3 %all-to-all-start = ((bf16[32,2048,32]{1,2,0:T(8,128)(2,1)}), bf16[32,2048,32]{1,2,0:T(8,128)(2,1)}, u32[]{:S(2)}, u32[]{:S(2)}) async-start(bf16[32,2048,32]{1,2,0:T(8,128)(2,1)} %bitcast_dynamic-update-slice_fusion), calls=%async_computation | async-start | bytes 8388608 | tf_op jit(solution)/shard_map/all_to_all | solution.py:16
  64.1 234.6 %all-reduce.3.cloned.1.call-start = ((), (), s32[]{:S(2)}) async-start(), calls=%async_computation.1 | async-start | bytes 4194304 | tf_op jit(solution)/shard_map/psum | solution.py:9
  158.0 2.8 copy-start.2
  168.9 285.0 %all-reduce.5.cloned.1.call-start = ((), (), s32[]{:S(2)}) async-start(), calls=%async_computation.2 | async-start | bytes 4194304 | tf_op jit(solution)/shard_map/psum | solution.py:9
  298.7 8.7 %copy-start = (bf16[1024,1024]{0,1:T(8,128)(2,1)S(1)}, bf16[1024,1024]{0,1:T(8,128)(2,1)}, u32[]{:S(2)}) copy-start(bf16[1024,1024]{0,1:T(8,128)(2,1)} %all-reduce.3.cloned.1.call-done) | copy-start | bytes 6291460
  453.9 13.3 %copy-start.1 = (bf16[1024,1024]{0,1:T(8,128)(2,1)S(1)}, bf16[1024,1024]{0,1:T(8,128)(2,1)}, u32[]{:S(2)}) copy-start(bf16[1024,1024]{0,1:T(8,128)(2,1)} %all-reduce.5.cloned.1.call-done) | copy-start | bytes 6291460
Sparse Core Ops, SparseCore 0:
  169.0 129.6 all-reduce.2
  314.4 139.4 all-reduce.4
